TPU v7x, 32 devices: a whole 2x2x4 slice. The times are simulated.
32 devices in a mesh: row: 4 (over z), col: 8 (over y, x, core).
Axes of the slice: x: 2, y: 2, z: 4, core: 2. Of those that a mesh axis runs over, the one named last changes fastest.
Arguments:
- right_side: float32 [2, 16, 512, 512], P(None, None, 'row', 'col'), may hold values from -12 to 12
- symbol: float32 [1024, 1024, 256], P('col', 'row'), may hold values from -0.25 to 4.75, as said below
Outputs:
- solution_field: float32 [2, 16, 512, 512], P(None, None, 'row', 'col')
- residual: float32 [2, 16, 512, 512], P(None, None, 'row', 'col')
Inputs may be any that keep to these rules, and one draw needn't show every extreme that they name: For each frequency pair (u, v) the 16 x 16 matrix with entries symbol[u, v, s * 16 + t] is symmetric and positive definite.
All inputs are finite; a program needn't handle non-finite values.
Results may differ from a plain program's by a relative error of at most 0.0003.
Values sent between devices are 32-bit elements; how exact they have to be, the bound alone decides.
A program may use at most 576 MiB of HBM per device.

v0:
```python
import math

import jax
import jax.numpy as jnp
from jax import lax
from jax.sharding import PartitionSpec as P

precise = lax.Precision.HIGHEST


def twiddle(out_index, in_index, length):
    product = out_index[:, None] * in_index[None, :] % length
    angle = product.astype(jnp.float32) * (2.0 * math.pi / length)
    return (jnp.cos(angle), jnp.sin(angle))


def widen(values):
    return values[:, None, None, None]


def squares(residual):
    return lax.psum(jnp.sum(residual * residual, axis=(1, 2, 3)), ("row", "col"))


def local(right_side, symbol):
    row_count = lax.axis_size("row")
    col_count = lax.axis_size("col")
    rhs_count, seg_count, row_block, col_block = right_side.shape
    rows_all = row_block * row_count
    cols_all = col_block * col_count
    freq_rows = 2 * rows_all
    freq_cols = 2 * cols_all
    blocks = symbol.reshape(symbol.shape[0], symbol.shape[1], seg_count, seg_count)
    rows_cos, rows_sin = twiddle(
        jnp.arange(freq_rows, dtype=jnp.int32), jnp.arange(rows_all, dtype=jnp.int32), freq_rows
    )
    cols_cos, cols_sin = twiddle(
        jnp.arange(freq_cols, dtype=jnp.int32), jnp.arange(cols_all, dtype=jnp.int32), freq_cols
    )
    back_cols_cos, back_cols_sin = (cols_cos.T, cols_sin.T)
    back_rows_cos, back_rows_sin = (rows_cos.T, rows_sin.T)
    norm_factor = 1.0 / (freq_rows * freq_cols)
    residual = right_side
    norm_now = squares(residual)
    whole_rows = lax.all_to_all(right_side, "row", split_axis=1, concat_axis=2, tiled=True)
    real_rows = jnp.einsum("ui,ksij->ksuj", rows_cos, whole_rows, precision=precise)
    imag_rows = -jnp.einsum("ui,ksij->ksuj", rows_sin, whole_rows, precision=precise)
    whole_cols = lax.all_to_all(
        jnp.stack([real_rows, imag_rows]), "col", split_axis=3, concat_axis=4, tiled=True
    )
    cos_part = jnp.einsum("vj,rksuj->rksuv", cols_cos, whole_cols, precision=precise)
    sin_part = jnp.einsum("vj,rksuj->rksuv", cols_sin, whole_cols, precision=precise)
    spectrum = jnp.stack([cos_part[0] + sin_part[1], cos_part[1] - sin_part[0]])
    all_segments = lax.all_to_all(spectrum, "row", split_axis=4, concat_axis=2, tiled=True)
    mixture = jnp.einsum("uvst,rktuv->rksuv", blocks, all_segments, precision=precise)
    own_segments = lax.all_to_all(mixture, "row", split_axis=2, concat_axis=4, tiled=True)
    cos_back = jnp.einsum("jv,rksuv->rksuj", back_cols_cos, own_segments, precision=precise)
    sin_back = jnp.einsum("jv,rksuv->rksuj", back_cols_sin, own_segments, precision=precise)
    inverted = jnp.stack([cos_back[0] - sin_back[1], sin_back[0] + cos_back[1]])
    freq_whole = lax.all_to_all(inverted, "col", split_axis=4, concat_axis=3, tiled=True)
    spatial = jnp.einsum("iu,ksuj->ksij", back_rows_cos, freq_whole[0], precision=precise)
    spatial = (
        spatial - jnp.einsum("iu,ksuj->ksij", back_rows_sin, freq_whole[1], precision=precise)
    ) * norm_factor
    returned = lax.all_to_all(spatial, "row", split_axis=2, concat_axis=1, tiled=True)
    curve = lax.psum(jnp.sum(right_side * returned, axis=(1, 2, 3)), ("row", "col"))
    step_size = widen(norm_now / curve)
    solution = step_size * right_side
    residual = residual - step_size * returned
    return (solution, residual)


def solution(mesh):
    placed = (P(None, None, "row", "col"), P("col", "row", None))
    return jax.shard_map(
        local,
        mesh=mesh,
        in_specs=placed,
        out_specs=(P(None, None, "row", "col"), P(None, None, "row", "col")),
        check_vma=False,
    )
```

profile of v0, /device:TPU:0, one launch (start us, length us, event | category | flops | bytes accessed | tf_op | source)
XLA Modules:
  0.0 1495.4 jit_solution(2727610797402067509)
XLA Ops:
  0.6 1.3 copy.43
  2.0 31.9 %all_to_all.105 = f32[2,16,128,64]{2,3,0,1:T(8,128)S(1)} all-to-all(f32[2,16,128,64]{2,3,0,1:T(8,128)S(1)} %copy.43), channel_id=1, replica_groups=mesh['row'=4,'col'=8] {'row'}, dimensions={1} | all-to-all | bytes 2097152 | tf_op jit(solution)/shard_map/all_to_all | solution.py:45
  33.8 0.7 copy.78
  34.5 0.4 all_to_all.79
  34.9 12.5 negate_bitcast_fusion
  47.5 12.7 fusion.24
  60.2 2.3 pad_maximum_fusion.1
  62.5 8.6 copy.45
  71.0 11.5 reshape.18
  82.5 53.7 %all_to_all.106 = f32[8,1,131072]{2,1,0:T(1,128)} all-to-all(f32[8,1,131072]{2,1,0:T(1,128)} %reshape.18), channel_id=1, replica_groups=mesh['row'=4,'col'=8] {'col'}, dimensions={0} | all-to-all | bytes 8388608 | tf_op jit(solution)/shard_map/all_to_all | solution.py:48
  136.3 0.5 broadcast.73
  136.8 13.7 reduce
  150.5 11.1 reshape.19
  161.6 8.5 copy.73
  170.1 0.0 copy-start.2
  170.1 38.7 %fusion.17 = f32[2,2,4,128,1024]{4,3,2,1,0:T(8,128)} fusion(f32[2,2,4,128,512]{3,4,2,1,0:T(8,128)} %bitcast.111), kind=kOutput, calls=%fused_computation.28 | convolution fusion | flops 12892241920 | bytes 12582912 | tf_op jit(solution)/shard_map/vj,rksuj->rksuv/dot_general | solution.py:52
  208.9 0.0 copy-done.2
  208.9 36.0 %fusion.5 = f32[2,2,4,128,1024]{4,3,2,1,0:T(8,128)} fusion(f32[2,2,4,128,512]{3,4,2,1,0:T(8,128)S(1)} %bitcast.112), kind=kOutput, calls=%fused_computation.16 | convolution fusion | flops 12892241920 | bytes 12582912 | tf_op jit(solution)/shard_map/vj,rksuj->rksuv/dot_general | solution.py:51
  244.9 10.3 slice_add_fusion
  255.2 6.7 pad_maximum_fusion
  261.9 10.2 copy.50
  272.1 5.6 all-to-all-start.2
  277.7 33.5 %copy.53 = f32[128,256,256]{1,2,0:T(8,128)} copy(f32[128,256,256]{2,1,0:T(8,128)} %param.3) | data formatting | bytes 67108864 | tf_op args[1]
  311.2 124.5 %copy.71 = f32[128,256,16,16,1]{3,2,4,1,0:T(8,128)} copy(f32[128,256,16,16,1]{1,3,2,0,4:T(8,128)} %bitcast.100) | data formatting | bytes 67108864 | tf_op jit(solution)/shard_map/reshape | solution.py:33
  435.6 24.8 %all-to-all-done.2 = f32[2,2,4,128,1024]{3,2,1,0,4:T(4,128)} async-done(((f32[2,2,4,128,1024]{3,2,1,0,4:T(4,128)}), f32[2,2,4,128,1024]{3,2,1,0,4:T(4,128)}, u32[]{:S(2)}, u32[]{:S(2)}) %all-to-all-start.2) | async-done | bytes 8388640 | tf_op jit(solution)/shard_map/all_to_all | solution.py:54
  460.5 9.3 copy.51
  469.8 9.9 copy.52
  479.7 52.4 %copy.54 = f32[2,2,16,128,256]{2,1,0,4,3:T(2,128)} copy(f32[2,2,16,128,256]{4,3,2,1,0:T(8,128)} %bitcast.101) | data formatting | bytes 16777216 | tf_op jit(solution)/shard_map/all_to_all | solution.py:54
  532.1 443.6 %convolution_bitcast_fusion = f32[2,2,16,128,256]{2,1,0,4,3:T(2,128)} fusion(f32[2,2,16,128,256]{2,1,0,4,3:T(2,128)} %copy.54, f32[128,256,16,16,1]{3,2,4,1,0:T(8,128)} %copy.71), kind=kOutput, calls=%fused_computation | convolution fusion | flops 402653184 | bytes 50331648 | tf_op jit(solution)/shard_map/uvst,rktuv->rksuv/dot_general | solution.py:55
  975.7 54.4 %copy.56 = f32[2,2,16,128,256]{4,3,1,0,2:T(8,128)} copy(f32[2,2,16,128,256]{2,1,0,4,3:T(2,128)} %convolution_bitcast_fusion) | data formatting | bytes 16777216 | tf_op jit(solution)/shard_map/uvst,rktuv->rksuv/transpose | solution.py:55
  1030.1 190.1 %all_to_all.107 = f32[2,2,16,128,256]{4,3,1,0,2:T(8,128)} all-to-all(f32[2,2,16,128,256]{4,3,1,0,2:T(8,128)} %copy.56), channel_id=1, replica_groups=mesh['row'=4,'col'=8] {'row'}, dimensions={2} | all-to-all | bytes 16777216 | tf_op jit(solution)/shard_map/all_to_all | solution.py:56
  1220.2 12.2 copy.58
  1232.3 10.7 all_to_all.91
  1243.1 0.0 copy-start.1
  1243.1 52.4 %fusion.15 = f32[2,2,4,128,512]{4,3,2,1,0:T(8,128)S(1)} fusion(f32[2,2,4,128,1024]{4,3,2,1,0:T(8,128)} %all_to_all.91), kind=kOutput, calls=%fused_computation.26 | convolution fusion | flops 12892241920 | bytes 12582912 | tf_op jit(solution)/shard_map/jv,rksuv->rksuj/dot_general | solution.py:58
  1295.5 0.0 copy-done.1
  1295.5 22.5 %fusion.3 = f32[2,2,4,128,512]{4,3,2,1,0:T(8,128)S(1)} fusion(f32[2,2,4,128,1024]{4,3,2,1,0:T(8,128)S(1)} %copy-done.1), kind=kOutput, calls=%fused_computation.14 | convolution fusion | flops 12892241920 | bytes 12582912 | tf_op jit(solution)/shard_map/jv,rksuv->rksuj/dot_general | solution.py:57
  1318.1 1.0 slice_subtract_fusion.1
  1319.1 2.4 pad_maximum_fusion.2
  1321.5 5.4 copy.59
  1326.9 52.9 %all_to_all.108 = f32[2,2,4,128,512]{3,2,1,0,4:T(4,128)S(1)} all-to-all(f32[2,2,4,128,512]{3,2,1,0,4:T(4,128)} %copy.59), channel_id=1, replica_groups=mesh['row'=4,'col'=8] {'col'}, dimensions={4} | all-to-all | bytes 8388608 | tf_op jit(solution)/shard_map/all_to_all | solution.py:60
  1379.8 1.3 copy.60
  1381.1 1.7 fusion.78
  1382.9 1.2 copy.62
  1384.1 1.5 squeeze.5
  1385.6 2.8 copy.61
  1388.4 1.5 squeeze.4
  1389.8 0.0 copy-start.3
  1389.8 13.4 fusion.7
  1403.3 0.0 copy-done.3
  1403.3 12.0 fusion.33
  1415.3 1.1 copy.63
  1416.4 2.0 reshape.20
  1418.4 28.1 %all_to_all.109 = f32[4,1,65536]{2,1,0:T(1,128)S(1)} all-to-all(f32[4,1,65536]{2,1,0:T(1,128)S(1)} %reshape.20), channel_id=1, replica_groups=mesh['row'=4,'col'=8] {'row'}, dimensions={0} | all-to-all | bytes 2097152 | tf_op jit(solution)/shard_map/all_to_all | solution.py:65
  1446.6 3.7 reduce.1
  1450.3 2.8 reshape.21
  1453.1 0.0 copy-start
  1453.1 1.9 copy.64
  1455.0 0.0 copy-done
  1455.0 0.4 multiply_reduce_fusion
  1455.4 37.8 %all-reduce = (f32[2]{0:T(128)S(1)}, f32[2]{0:T(128)S(1)}) all-reduce(f32[2]{0:T(128)S(1)} %get-tuple-element.3, f32[2]{0:T(128)S(1)} %get-tuple-element.2), channel_id=1, replica_groups=mesh['row'=4,'col'=8] {'row','col'}, use_global_device_ids=true, to_apply=%region_1.2 | all-reduce | flops 4 | bytes 32 | tf_op jit(solution)/shard_map/psum | solution.py:22
  1493.3 1.6 multiply_subtract_fusion
  (1 shorter events, 0.0 us)
Async XLA Ops:
  170.1 38.8 %copy-start.2 = (f32[2,2,4,8,128,64]{4,5,3,2,1,0:T(8,128)S(1)}, f32[2,2,4,8,128,64]{4,5,3,2,1,0:T(8,128)}, u32[]{:S(2)}) copy-start(f32[2,2,4,8,128,64]{4,5,3,2,1,0:T(8,128)} %copy.73) | copy-start | bytes 12582916
  272.1 188.4 %all-to-all-start.2 = ((f32[2,2,4,128,1024]{3,2,1,0,4:T(4,128)}), f32[2,2,4,128,1024]{3,2,1,0,4:T(4,128)}, u32[]{:S(2)}, u32[]{:S(2)}) async-start(f32[2,2,4,128,1024]{3,2,1,0,4:T(4,128)} %copy.50), calls=%async_computation.2 | async-start | bytes 16777216 | tf_op jit(solution)/shard_map/all_to_all | solution.py:54
  1243.1 52.5 %copy-start.1 = (f32[2,2,4,128,1024]{4,3,2,1,0:T(8,128)S(1)}, f32[2,2,4,128,1024]{4,3,2,1,0:T(8,128)}, u32[]{:S(2)}) copy-start(f32[2,2,4,128,1024]{4,3,2,1,0:T(8,128)} %all_to_all.91) | copy-start | bytes 25165828
  1389.8 13.4 copy-start.3
  1453.1 2.0 copy-start
where the time goes:
time: 1510 us; the launch traced here: 1500 us
  matrix products  644 us (43%)
  blocking collectives  395 us (26%)
  local copies, waits for them, and re-layouts  383 us (25%)
  other arithmetic  42 us (3%)
  waiting for transfers between devices  24.8 us (2%)
    dot_general x1, matrix products, local(): jnp.einsum('uvst,rktuv->rksuv', blocks, all_segments, precision=precise)  444 us
    all_to_all x1, blocking collectives, local(): lax.all_to_all(mixture, 'row', split_axis=2, concat_axis=4, tiled=True)  190 us
    reshape x1, local copies, waits for them, and re-layouts, local(): symbol.reshape(symbol.shape[0], symbol.shape[1], seg_count, seg_count)  124 us
    all_to_all x3, local copies, waits for them, and re-layouts, local(): lax.all_to_all(spectrum, 'row', split_axis=4, concat_axis=2, tiled=True)  71.6 us
    unnamed x14, local copies, waits for them, and re-layouts  62.3 us
    transpose x1, local copies, waits for them, and re-layouts, local(): jnp.einsum('uvst,rktuv->rksuv', blocks, all_segments, precision=precise)  54.4 us
    all_to_all x1, blocking collectives, local(): lax.all_to_all(jnp.stack([real_rows, imag_rows]), 'col', split_axis=3, co...  53.7 us
    all_to_all x1, blocking collectives, local(): lax.all_to_all(inverted, 'col', split_axis=4, concat_axis=3, tiled=True)  52.9 us
  transfers between devices with their start and end apart: 1, of which 1 were waited for; matrix products, arithmetic and copies ran while one was open for 11% of the time, Pallas kernels for 0%

commit v1 on v0

v1 whole, which is shorter than its diff:
```python
import math

import jax
import jax.numpy as jnp
from jax import lax
from jax.experimental import pallas as pl
from jax.experimental.pallas import tpu as pltpu
from jax.sharding import PartitionSpec as P

PRECISION = lax.Precision.HIGH
ROW_STEP = 8


def tables(phase, length):
    angle = (phase % length).astype(jnp.float32) * (2.0 * math.pi / length)
    return lax.optimization_barrier((jnp.cos(angle), jnp.sin(angle)))


def steps(count, stride=1):
    return jnp.arange(count, dtype=jnp.int32) * stride


def row_transform(freq_rows, rows_all, freq_block):
    fine = math.gcd(32, freq_block)
    place = jnp.tile(steps(rows_all), 2)
    part_in = jnp.repeat(steps(2), rows_all)
    coarse_cos, coarse_sin = tables(steps(freq_rows // fine, fine)[:, None] * place[None, :], freq_rows)
    quarter = (steps(2)[:, None] - part_in[None, :]) * (freq_rows // 4) + freq_rows
    fine_cos, fine_sin = tables(
        steps(fine)[None, :, None] * place[None, None, :] + quarter[:, None, :], freq_rows
    )
    shape = (freq_rows // freq_block, 1, freq_block // fine, 1, 2 * rows_all)
    coarse_cos, coarse_sin = coarse_cos.reshape(shape), coarse_sin.reshape(shape)
    fine_cos, fine_sin = fine_cos[None, :, None], fine_sin[None, :, None]
    return (coarse_cos * fine_cos - coarse_sin * fine_sin).reshape(2 * freq_rows, 2 * rows_all)


def col_transform(freq_cols, cols_all, freq_block, first):
    fine = math.gcd(16, cols_all)
    freq = first + steps(freq_block)
    coarse_cos, coarse_sin = tables(steps(cols_all // fine, fine)[:, None] * freq[None, :], freq_cols)
    quarter = steps(2, freq_cols // 4)[:, None, None]
    fine_cos, fine_sin = tables(steps(fine)[None, :, None] * freq[None, None, :] + quarter, freq_cols)
    coarse_cos, coarse_sin = coarse_cos[None, :, None], coarse_sin[None, :, None]
    fine_cos, fine_sin = fine_cos[:, None], fine_sin[:, None]
    return (coarse_cos * fine_cos - coarse_sin * fine_sin).reshape(2, cols_all, freq_block)


def mix(symbol, spectrum, rhs_count, seg_count):
    freq_rows, freq_cols, pair_count = symbol.shape
    devices, parts, _, width = spectrum.shape
    held = width // freq_cols
    step = math.gcd(ROW_STEP, freq_rows)

    def body(symbol_ref, in_ref, out_ref, turned):
        def one(u, carry):
            turned[...] = symbol_ref[u].T
            sums = {}
            for t in range(seg_count):
                column = turned[t * seg_count : (t + 1) * seg_count, :]
                for part in range(parts):
                    for k in range(rhs_count):
                        owner, at = divmod(k * seg_count + t, held)
                        line = in_ref[owner, part, pl.ds(u, 1), at * freq_cols : (at + 1) * freq_cols]
                        term = column * line
                        sums[part, k] = sums[part, k] + term if t else term
            for part in range(parts):
                for k in range(rhs_count):
                    for s in range(seg_count):
                        owner, at = divmod(k * seg_count + s, held)
                        out_ref[owner, part, pl.ds(u, 1), at * freq_cols : (at + 1) * freq_cols] = sums[
                            part, k
                        ][s : s + 1, :]
            return carry

        lax.fori_loop(0, step, one, 0)

    block = pl.BlockSpec((devices, parts, step, width), lambda i: (0, 0, i, 0))
    return pl.pallas_call(
        body,
        grid=(freq_rows // step,),
        in_specs=[pl.BlockSpec((step, freq_cols, pair_count), lambda i: (i, 0, 0)), block],
        out_specs=block,
        out_shape=jax.ShapeDtypeStruct(spectrum.shape, jnp.float32),
        scratch_shapes=[pltpu.VMEM((pair_count, freq_cols), jnp.float32)],
        name="mix",
    )(symbol, spectrum)


def local(right_side, symbol):
    row_count = lax.axis_size("row")
    col_count = lax.axis_size("col")
    rhs_count, seg_count, row_block, col_block = right_side.shape
    freq_block, freq_width = symbol.shape[:2]
    rows_all = row_block * row_count
    cols_all = col_block * col_count
    freq_rows = freq_block * col_count
    freq_cols = freq_width * row_count
    fields = rhs_count * seg_count
    held = fields // col_count
    to_rows = row_transform(freq_rows, rows_all, freq_block)
    to_cols = col_transform(freq_cols, cols_all, freq_width, lax.axis_index("row") * freq_width)
    flat = right_side.reshape(fields, row_block, col_block)
    whole_cols = lax.all_to_all(flat, "col", split_axis=0, concat_axis=2, tiled=True)
    whole = lax.all_gather(whole_cols, "row", axis=1, tiled=True)
    half = jnp.einsum("prc,zcv->zrpv", whole, to_cols, precision=PRECISION)
    half = half.reshape(2 * rows_all, held * freq_width)
    spectrum = jnp.dot(to_rows, half, precision=PRECISION)
    spectrum = spectrum.reshape(col_count, 2, freq_block, held * freq_width)
    spectrum = lax.all_to_all(spectrum, "col", split_axis=0, concat_axis=0, tiled=True)
    mixed = mix(symbol, spectrum, rhs_count, seg_count)
    mixed = lax.all_to_all(mixed, "col", split_axis=0, concat_axis=0, tiled=True)
    mixed = mixed.reshape(2 * freq_rows, held * freq_width)
    back = lax.dot_general(to_rows, mixed, (((0,), (0,)), ((), ())), precision=PRECISION)
    back = back.reshape(2, rows_all, held, freq_width)
    image = jnp.einsum("zrpv,zcv->prc", back, to_cols, precision=PRECISION)
    image = lax.psum_scatter(image, "row", scatter_dimension=1, tiled=True)
    applied = lax.all_to_all(image, "col", split_axis=2, concat_axis=0, tiled=True)
    applied = applied.reshape(right_side.shape) * (1.0 / (freq_rows * freq_cols))
    norm_now, curve = lax.psum(
        (
            jnp.sum(right_side * right_side, axis=(1, 2, 3)),
            jnp.sum(right_side * applied, axis=(1, 2, 3)),
        ),
        ("row", "col"),
    )
    step_size = (norm_now / curve)[:, None, None, None]
    return (step_size * right_side, right_side - step_size * applied)


def solution(mesh):
    placed = P(None, None, "row", "col")
    return jax.shard_map(
        local,
        mesh=mesh,
        in_specs=(placed, P("col", "row", None)),
        out_specs=(placed, placed),
        check_vma=False,
    )
```

time: 1510 us -> 559 us (0.37)
  matrix products: 644 us -> 54.8 us
  local copies, waits for them, and re-layouts: 383 us -> 38.1 us
  blocking collectives: 395 us -> 177 us
  waiting for transfers between devices: 24.8 us -> 232 us
  other arithmetic: 42 us -> 8.67 us
  Pallas kernels: 0 us -> 28.7 us
    dot_general x9 -> x4, matrix products: 644 us -> 54.8 us  [the longest x1 21.6 us: local(): spectrum = jnp.dot(to_rows, half, precision=PRECISION)]
    all_to_all x5 -> x3, blocking collectives: 357 us -> 137 us  [the longest x1 97.5 us: local(): lax.all_to_all(spectrum, 'col', split_axis=0, concat_axis=0, tiled=True)]
    reshape x1, local copies, waits for them, and re-layouts: 124 us -> 5.77 us  [local(): half = half.reshape(2 * rows_all, held * freq_width)]
    all_to_all x11 -> x3, local copies, waits for them, and re-layouts: 108 us -> 1.51 us  [the longest x2 1.38 us: local(): lax.all_to_all(flat, 'col', split_axis=0, concat_axis=2, tiled=True)]
    all_gather x0 -> x1, waiting for transfers between devices: none -> 77.7 us  [local(): whole = lax.all_gather(whole_cols, 'row', axis=1, tiled=True)]
    reduce_scatter x0 -> x1, waiting for transfers between devices: none -> 73.6 us  [local(): image = lax.psum_scatter(image, 'row', scatter_dimension=1, tiled=True)]
    unnamed x14 -> x6, local copies, waits for them, and re-layouts: 62.3 us -> 0.02 us
    all_to_all x1, waiting for transfers between devices: 24.8 us -> 80.3 us  [local(): lax.all_to_all(mixed, 'col', split_axis=0, concat_axis=0, tiled=True)]
  transfers between devices with their start and end apart: 1 -> 3, of which waited for: 1 -> 3; matrix products, arithmetic and copies ran while one was open for 11% -> 3% of each run, Pallas kernels for 0% -> 0%
where the time goes in v1:
time: 559 us; the launch traced here: 558 us
  waiting for transfers between devices  232 us (42%)
  blocking collectives  177 us (32%)
  matrix products  54.8 us (10%)
  local copies, waits for them, and re-layouts  38.1 us (7%)
  Pallas kernels  28.7 us (5%)
  between operations  14.3 us (3%)
  other arithmetic  8.67 us (2%)
    all_to_all x1, blocking collectives, local(): lax.all_to_all(spectrum, 'col', split_axis=0, concat_axis=0, tiled=True)  97.5 us
    all_to_all x1, waiting for transfers between devices, local(): lax.all_to_all(mixed, 'col', split_axis=0, concat_axis=0, tiled=True)  80.3 us
    all_gather x1, waiting for transfers between devices, local(): whole = lax.all_gather(whole_cols, 'row', axis=1, tiled=True)  77.7 us
    reduce_scatter x1, waiting for transfers between devices, local(): image = lax.psum_scatter(image, 'row', scatter_dimension=1, tiled=True)  73.6 us
    psum x1, blocking collectives, local(): lax.psum((jnp.sum(right_side * right_side, axis=(1, 2, 3)), jnp.sum(right...  39.8 us
    pallas_call x1, Pallas kernels, mix(): pl.pallas_call(body, grid=(freq_rows // step,), in_specs=[pl.BlockSpec((s...  28.7 us
    dot_general x1, matrix products, local(): spectrum = jnp.dot(to_rows, half, precision=PRECISION)  21.6 us
    all_to_all x1, blocking collectives, local(): lax.all_to_all(flat, 'col', split_axis=0, concat_axis=2, tiled=True)  20.5 us
  transfers between devices with their start and end apart: 3, of which 3 were waited for; matrix products, arithmetic and copies ran while one was open for 3% of the time, Pallas kernels for 0%

profile of v1, /device:TPU:0, one launch (start us, length us, event | category | flops | bytes accessed | tf_op | source)
XLA Modules:
  0.0 558.0 jit_solution(7428121474630804757)
XLA Ops:
  7.2 0.0 all-gather.2.cloned.1.call-start
  7.2 20.5 %all_to_all.43 = f32[32,128,64]{1,2,0:T(8,128)S(1)} all-to-all(f32[32,128,64]{1,2,0:T(8,128)} %bitcast.80), channel_id=1, replica_groups=mesh['row'=4,'col'=8] {'col'}, dimensions={0} | all-to-all | bytes 2097152 | tf_op jit(solution)/shard_map/all_to_all | solution.py:104
  27.7 0.1 copy.22
  27.8 1.3 copy.23
  29.1 0.0 all-gather.2.cloned.1.call-update
  29.2 0.2 fusion.36
  29.5 0.2 fusion.38
  29.7 0.6 fusion.28
  30.4 1.0 fusion.26
  31.5 0.1 fusion.19
  31.7 77.7 %all-gather.2.cloned.1.call-done = f32[4,512,512]{2,1,0:T(8,128)} async-done(((f32[4,128,512]{2,1,0:T(8,128)}), f32[4,512,512]{2,1,0:T(8,128)}) %all-gather.2.cloned.1.call-update) | async-done | bytes 4194320 | tf_op jit(solution)/shard_map/all_gather | solution.py:105
  109.4 10.7 %fusion.11 = f32[2,512,4,256]{1,3,2,0:T(8,128)} fusion(f32[4,512,512]{2,1,0:T(8,128)} %all-gather.2.cloned.1.call-done, f32[2,512,256]{2,1,0:T(8,128)S(1)} %fusion.19), kind=kOutput, calls=%fused_computation.12 | convolution fusion | flops 3221225472 | bytes 9437184 | tf_op jit(solution)/shard_map/prc,zcv->zrpv/dot_general | solution.py:106
  120.1 5.3 copy.25
  125.3 5.8 %reshape.160 = f32[1024,1024,1,1]{1,0,2,3:T(8,128)} reshape(f32[2,512,4,256]{3,2,1,0:T(4,128)} %copy.25) | data formatting | bytes 8388608 | tf_op jit(solution)/shard_map/reshape | solution.py:107
  131.1 0.1 mul.346
  131.2 0.1 mul.353
  131.3 2.5 mul.350
  133.9 2.5 mul.343
  136.3 21.6 %fusion = f32[8,2,128,1024]{3,2,1,0:T(8,128)S(1)} fusion(f32[1024,1024,1,1]{1,0,2,3:T(8,128)} %reshape.160, f32[2,128,1024]{2,1,0:T(8,128)S(1)} %bitcast.93, f32[8,128,1024]{2,1,0:T(8,128)} %bitcast.85, f32[2,128,1024]{2,1,0:T(8,128)S(1)} %bitcast.92, f32[8,128,1024]{2,1,0:T(8,128)} %bitcast.86), kind=kOutput, calls=%fused_computation | convolution fusion | flops 12891193344 | bytes 23068672 | tf_op jit(solution)/shard_map/dot_general | solution.py:108
  158.0 97.5 %all_to_all.44.in_ref = f32[8,2,128,1024]{3,2,1,0:T(8,128)} all-to-all(f32[8,2,128,1024]{3,2,1,0:T(8,128)S(1)} %fusion), channel_id=1, replica_groups=mesh['row'=4,'col'=8] {'col'}, dimensions={0} | all-to-all | bytes 16777216 | tf_op jit(solution)/shard_map/all_to_all | solution.py:110
  255.5 28.7 %mix.1 = f32[8,2,128,1024]{3,2,1,0:T(8,128)} custom-call(f32[128,256,256]{2,1,0:T(8,128)} %symbol_ref.1, f32[8,2,128,1024]{3,2,1,0:T(8,128)} %all_to_all.44.in_ref), custom_call_target="tpu_custom_call" | custom-call | tf_op jit(solution)/shard_map/mix/pallas_call | solution.py:79
  284.2 4.9 all-to-all-start.2
  289.1 0.0 reduce-scatter.2.cloned.1.call-start
  289.2 4.5 multiply_subtract_fusion
  293.7 9.2 %copy.34 = f32[1024,2048]{1,0:T(8,128)} copy(f32[1024,2048]{0,1:T(8,128)} %bitcast.79) | data formatting | bytes 16777216 | tf_op jit(solution)/shard_map/dot_general | solution.py:114
  302.8 80.3 %all-to-all-done.2 = f32[8,2,128,1024]{3,2,1,0:T(8,128)} async-done(((f32[8,2,128,1024]{3,2,1,0:T(8,128)}), f32[8,2,128,1024]{3,2,1,0:T(8,128)}, u32[]{:S(2)}, u32[]{:S(2)}) %all-to-all-start.2) | async-done | bytes 8388640 | tf_op jit(solution)/shard_map/all_to_all | solution.py:112
  383.2 9.1 %copy.26 = f32[1024,2048]{1,0:T(8,128)} copy(f32[1024,2048]{0,1:T(8,128)} %bitcast.22) | data formatting | bytes 16777216 | tf_op jit(solution)/shard_map/dot_general | solution.py:114
  392.3 17.3 %fusion.40 = f32[2,512,4,256]{3,1,0,2:T(8,128)S(1)} fusion(f32[2,512,2048,1]{2,1,0,3:T(8,128)} %bitcast.83, f32[4,256,2048,1]{2,1,3,0:T(8,128)} %bitcast.84), kind=kOutput, calls=%fused_computation.76 | convolution fusion | flops 12884901888 | bytes 20971520 | tf_op jit(solution)/shard_map/dot_general | solution.py:114
  409.6 0.0 copy-start
  409.6 5.3 convolution_bitcast_fusion
  414.9 0.0 reduce-scatter.2.cloned.1.call-update
  414.9 73.6 %reduce-scatter.2.cloned.1.call-done = f32[4,128,512]{1,2,0:T(8,128)} async-done(((f32[4,512,512]{1,2,0:T(8,128)}), f32[4,128,512]{1,2,0:T(8,128)}) %reduce-scatter.2.cloned.1.call-update) | async-done | bytes 1048592 | tf_op jit(solution)/shard_map/reduce_scatter | solution.py:117
  488.6 1.9 copy.28
  490.5 18.8 %all_to_all.45 = f32[4,128,512]{1,0,2:T(4,128)S(1)} all-to-all(f32[4,128,512]{1,0,2:T(4,128)S(1)} %copy.28), channel_id=1, replica_groups=mesh['row'=4,'col'=8] {'col'}, dimensions={2} | all-to-all | bytes 2097152 | tf_op jit(solution)/shard_map/all_to_all | solution.py:118
  509.2 0.1 copy.29
  509.4 0.0 copy-done
  509.4 0.4 fusion.16
  509.8 39.8 %all-reduce = (f32[2]{0:T(128)S(1)}, f32[2]{0:T(128)S(1)}) all-reduce(f32[2]{0:T(128)S(1)} %get-tuple-element.19, f32[2]{0:T(128)S(1)} %get-tuple-element.18), channel_id=1, replica_groups=mesh['row'=4,'col'=8] {'row','col'}, use_global_device_ids=true, to_apply=%region_1.2 | all-reduce | flops 4 | bytes 32 | tf_op jit(solution)/shard_map/psum | solution.py:120
  549.5 1.6 fusion.17
  (16 shorter events, 0.2 us)
Async XLA Ops:
  7.2 102.2 %all-gather.2.cloned.1.call-start = ((), (), s32[]{:S(2)}) async-start(), calls=%async_computation.5 | async-start | bytes 5242880 | tf_op jit(solution)/shard_map/all_gather | solution.py:105
  284.2 99.0 %all-to-all-start.2 = ((f32[8,2,128,1024]{3,2,1,0:T(8,128)}), f32[8,2,128,1024]{3,2,1,0:T(8,128)}, u32[]{:S(2)}, u32[]{:S(2)}) async-start(f32[8,2,128,1024]{3,2,1,0:T(8,128)} %mix.1), calls=%async_computation.2 | async-start | bytes 16777216 | tf_op jit(solution)/shard_map/all_to_all | solution.py:112
  289.1 199.4 %reduce-scatter.2.cloned.1.call-start = ((), (), s32[]{:S(2)}) async-start(), calls=%async_computation.6 | async-start | bytes 5242880 | tf_op jit(solution)/shard_map/reduce_scatter | solution.py:117
  409.6 99.8 %copy-start = (f32[2,16,128,64]{2,3,1,0:T(8,128)S(1)}, f32[2,16,128,64]{2,3,1,0:T(8,128)}, u32[]{:S(2)}) copy-start(f32[2,16,128,64]{2,3,1,0:T(8,128)} %param.2) | copy-start | bytes 3145732
Sparse Core Ops, SparseCore 0:
  29.3 80.0 all-gather.1
  415.0 73.4 reduce-scatter.1
